TPU v7x, 32 devices: a whole 2x2x4 slice. The times are simulated.
32 devices in a mesh: ctx: 8 (over y, x, core), dp: 4 (over z).
Axes of the slice: x: 2, y: 2, z: 4, core: 2. Of those that a mesh axis runs over, the one named last changes fastest.
Arguments:
- hidden_in: bfloat16 [4, 2048, 2048], P('dp', 'ctx'), may hold values from -6 to 6
- queries: bfloat16 [4, 2048, 2048], P('dp', 'ctx'), may hold values from -1000 to 1000
- norm_gain: bfloat16 [2048], replicated, may hold values from 0.099609375 to 1.8984375
- weight_store: bfloat16 [4, 2048, 512], P('dp', 'ctx'), may hold values from -0.125 to 0.125
- owners: int32 [2], replicated, may hold values from 0 to 3, as said below
- doc_lengths: int32 [4, 4], P('dp'), may hold values from 1 to 1024, 2048 in all within a row
Outputs:
- attended: bfloat16 [4, 2048, 2048], P('dp', 'ctx')
Inputs may be any that keep to these rules, and one draw needn't show every extreme that they name: `owners`: two different data ranks, one of them the last rank 4 - 1; the first owns the key projection, the second the value projection.
All inputs are finite; a program needn't handle non-finite values.
Results may differ from a plain program's by a relative error of at most 0.012.
Values may be sent and summed in bfloat16 or wider, within the bound.
No kernel may reach another device: no remote copies, remote signals or barrier semaphores. Data moves between devices by JAX's collectives and lax.ppermute only.
A program may use at most 64 MiB of HBM per device.

v0:
```python
import jax
import jax.numpy as jnp
from jax import lax
from jax.sharding import PartitionSpec as P

HS = 128
REACH = 4


def from_root(block, axis, owner):
    block = jnp.where(lax.axis_index(axis) == owner, block, jnp.zeros_like(block))
    return lax.psum(block, axis)


def from_behind(x, axis, by):
    size = lax.axis_size(axis)
    pairs = [(i, i + by) for i in range(size) if 0 <= i + by < size]
    return lax.ppermute(x, axis, pairs)


def find_starts(lengths, positions):
    ends = jnp.cumsum(lengths)
    starts = ends - lengths
    below = starts[None, :] <= positions[:, None]
    return jnp.max(jnp.where(below, starts[None, :], 0), axis=1)


def copy_owner(slot_rows, owner):
    return from_root(slot_rows, "dp", owner)


def local(hidden_in, queries, norm_gain, weight_store, owners, doc_lengths):
    tok_rows = hidden_in.shape[1]
    key_width = weight_store.shape[2]
    kv_heads = key_width // HS
    group = queries.shape[2] // key_width
    width_all = (REACH + 1) * tok_rows
    ctx_index = lax.axis_index("ctx")
    xf = hidden_in[0].astype(jnp.float32)
    scaled = (
        xf
        * lax.rsqrt(jnp.mean(xf * xf, axis=-1, keepdims=True) + 1e-05)
        * norm_gain.astype(jnp.float32)
    ).astype(jnp.bfloat16)
    own_slot = weight_store[0]
    key_part = copy_owner(own_slot, owners[0])
    value_part = copy_owner(own_slot, owners[1])
    key_sum = jnp.dot(
        scaled,
        lax.all_gather(key_part, "ctx", axis=0, tiled=True),
        preferred_element_type=jnp.float32,
    )
    value_sum = jnp.dot(
        scaled,
        lax.all_gather(value_part, "ctx", axis=0, tiled=True),
        preferred_element_type=jnp.float32,
    )
    kv_own = jnp.stack([key_sum.astype(jnp.bfloat16), value_sum.astype(jnp.bfloat16)])
    earlier = [from_behind(kv_own, "ctx", back) for back in range(REACH, 0, -1)]
    window = jnp.concatenate(earlier + [kv_own], axis=1)
    q_pos = ctx_index * tok_rows + jnp.arange(tok_rows, dtype=jnp.int32)
    k_pos = (ctx_index - REACH) * tok_rows + jnp.arange(width_all, dtype=jnp.int32)
    q_start = find_starts(doc_lengths[0], q_pos)
    allowed = (k_pos[None, :] >= q_start[:, None]) & (k_pos[None, :] <= q_pos[:, None])
    q_heads = jnp.transpose(queries[0].reshape(tok_rows, kv_heads, group, HS), (1, 2, 0, 3))
    k_heads = jnp.transpose(window[0].reshape(width_all, kv_heads, HS), (1, 0, 2))
    v_heads = jnp.transpose(window[1].reshape(width_all, kv_heads, HS), (1, 0, 2))
    inverse_root = 1.0 / jnp.sqrt(jnp.float32(HS))

    def one_head(args):
        q_one, k_one, v_one = args
        rows = q_one.reshape(group * tok_rows, HS)
        score = jnp.dot(rows, k_one.T, preferred_element_type=jnp.float32)
        score = score.reshape(group, tok_rows, width_all) * inverse_root
        score = jnp.where(allowed[None], score, jnp.float32(-1e30))
        top = jnp.max(score, axis=-1, keepdims=True)
        weight = jnp.exp(score - top)
        total = jnp.sum(weight, axis=-1)
        weight_b = weight.astype(jnp.bfloat16).reshape(group * tok_rows, width_all)
        summed = jnp.dot(weight_b, v_one, preferred_element_type=jnp.float32)
        summed = summed.reshape(group, tok_rows, HS)
        return (summed / total[..., None]).astype(jnp.bfloat16)

    outputs = lax.map(one_head, (q_heads, k_heads, v_heads))
    attended = jnp.transpose(outputs, (2, 0, 1, 3)).reshape(1, tok_rows, kv_heads * group * HS)
    return attended


def solution(mesh):
    return jax.shard_map(
        local,
        mesh=mesh,
        in_specs=(
            P("dp", "ctx", None),
            P("dp", "ctx", None),
            P(),
            P("dp", "ctx", None),
            P(),
            P("dp", None),
        ),
        out_specs=P("dp", "ctx", None),
        check_vma=False,
    )
```

profile of v0, /device:TPU:1, one launch (start us, length us, event | category | flops | bytes accessed | tf_op | source)
XLA Modules:
  0.0 198.7 jit_solution(8778680894563662250)
XLA Ops:
  6.5 1.4 fusion.36
  9.3 1.8 select_bitcast_fusion.1
  11.1 39.7 %all-reduce.3.cloned.1.call-done = (bf16[256,512]{1,0:T(8,128)(2,1)}, bf16[256,512]{1,0:T(8,128)(2,1)}) async-done(((bf16[256,512]{1,0:T(8,128)(2,1)}, bf16[256,512]{1,0:T(8,128)(2,1)}), (bf16[256,512]{1,0:T(8,128)(2,1)}, bf16[256,512]{1,0:T(8,128)(2,1)})) %all-reduce.3.cloned.1.call-update) | async-done | bytes 524304 | tf_op jit(solution)/shard_map/psum | solution.py:12
  53.4 28.6 %all-gather.3.cloned.1.call-done = bf16[2048,512]{1,0:T(8,128)(2,1)} async-done(((bf16[256,512]{1,0:T(8,128)(2,1)}), bf16[2048,512]{1,0:T(8,128)(2,1)}) %all-gather.3.cloned.1.call-update) | async-done | bytes 2097168 | tf_op jit(solution)/shard_map/all_gather | solution.py:50
  82.0 2.3 %fusion.30 = bf16[1,256,512]{2,1,0:T(8,128)(2,1)S(1)} fusion(bf16[2048,512]{1,0:T(8,128)(2,1)} %all-gather.3.cloned.1.call-done, bf16[1,256,2048]{2,1,0:T(8,128)(2,1)S(1)} %copy-done, f32[2048]{0:T(1024)S(1)} %convert_element_type.26, f32[256]{0:T(256)S(1)} %add_rsqrt_fusion), kind=kOutput, calls=%fused_computation.29 | convolution fusion | flops 539099136 | bytes 3417088 | tf_op jit(solution)/shard_map/dot_general | solution.py:48
  84.4 27.5 %all-gather.5.cloned.1.call-done = bf16[2048,512]{1,0:T(8,128)(2,1)} async-done(((bf16[256,512]{1,0:T(8,128)(2,1)}), bf16[2048,512]{1,0:T(8,128)(2,1)}) %all-gather.5.cloned.1.call-update) | async-done | bytes 2097168 | tf_op jit(solution)/shard_map/all_gather | solution.py:55
  111.8 2.3 %fusion.31 = bf16[1,256,512]{2,1,0:T(8,128)(2,1)S(1)} fusion(bf16[2048,512]{1,0:T(8,128)(2,1)} %all-gather.5.cloned.1.call-done, bf16[1,256,2048]{2,1,0:T(8,128)(2,1)S(1)} %copy-done, f32[2048]{0:T(1024)S(1)} %convert_element_type.26, f32[256]{0:T(256)S(1)} %add_rsqrt_fusion), kind=kOutput, calls=%fused_computation.30 | convolution fusion | flops 539099136 | bytes 3417088 | tf_op jit(solution)/shard_map/dot_general | solution.py:53
  115.7 3.8 %collective-permute-start = (bf16[2,256,512]{2,1,0:T(8,128)(2,1)}, bf16[2,256,512]{2,1,0:T(8,128)(2,1)}, u32[]{:S(2)}, u32[]{:S(2)}) collective-permute-start(bf16[2,256,512]{2,1,0:T(8,128)(2,1)} %pad_maximum_fusion), channel_id=1, source_target_pairs={{0,16},{4,20},{8,24},{12,28},{1,17},{5,21},{9,25},{13,29},{2,18},{... | collective-permute-start | bytes 1572872 | tf_op jit(solution)/shard_map/ppermute | solution.py:18
  119.5 2.1 %collective-permute-start.1 = (bf16[2,256,512]{2,1,0:T(8,128)(2,1)}, bf16[2,256,512]{2,1,0:T(8,128)(2,1)}, u32[]{:S(2)}, u32[]{:S(2)}) collective-permute-start(bf16[2,256,512]{2,1,0:T(8,128)(2,1)} %pad_maximum_fusion), channel_id=1, source_target_pairs={{0,12},{4,16},{8,20},{12,24},{16,28},{1,13},{5,17},{9,21},{13,25},... | collective-permute-start | bytes 1572872 | tf_op jit(solution)/shard_map/ppermute | solution.py:18
  121.6 2.9 %collective-permute-start.2 = (bf16[2,256,512]{2,1,0:T(8,128)(2,1)}, bf16[2,256,512]{2,1,0:T(8,128)(2,1)}, u32[]{:S(2)}, u32[]{:S(2)}) collective-permute-start(bf16[2,256,512]{2,1,0:T(8,128)(2,1)} %pad_maximum_fusion), channel_id=1, source_target_pairs={{0,8},{4,12},{8,16},{12,20},{16,24},{20,28},{1,9},{5,13},{9,17},{1... | collective-permute-start | bytes 1572872 | tf_op jit(solution)/shard_map/ppermute | solution.py:18
  124.5 1.9 collective-permute-start.3
  127.1 25.4 %collective-permute-done = bf16[2,256,512]{2,1,0:T(8,128)(2,1)} collective-permute-done((bf16[2,256,512]{2,1,0:T(8,128)(2,1)}, bf16[2,256,512]{2,1,0:T(8,128)(2,1)}, u32[]{:S(2)}, u32[]{:S(2)}) %collective-permute-start) | collective-permute-done | bytes 524320 | tf_op jit(solution)/shard_map/ppermute | solution.py:18
  153.6 5.2 %collective-permute-done.1 = bf16[2,256,512]{2,1,0:T(8,128)(2,1)} collective-permute-done((bf16[2,256,512]{2,1,0:T(8,128)(2,1)}, bf16[2,256,512]{2,1,0:T(8,128)(2,1)}, u32[]{:S(2)}, u32[]{:S(2)}) %collective-permute-start.1) | collective-permute-done | bytes 524320 | tf_op jit(solution)/shard_map/ppermute | solution.py:18
  163.4 3.6 %reshape_squeeze.10 = bf16[1280,4,128]{2,1,0:T(4,128)(2,1)} reshape(bf16[1,1280,512]{2,1,0:T(8,128)(2,1)} %get-tuple-element.96) | data formatting | bytes 2621440 | tf_op jit(solution)/shard_map/reshape;squeeze | solution.py:66
  168.2 3.1 %copy_bitcast_fusion = (bf16[4,1280,128]{2,1,0:T(8,128)(2,1)}, bf16[4,1280,128]{2,1,0:T(8,128)(2,1)S(1)}) fusion(bf16[1280,4,128]{2,1,0:T(4,128)(2,1)} %reshape_squeeze.11, bf16[1280,4,128]{2,1,0:T(4,128)(2,1)} %reshape_squeeze.10), kind=kLoop, calls=%fused_computation.25 | loop fusion | bytes 5242880 | tf_op jit(solution)/shard_map/transpose | solution.py:67
  171.3 18.5 %while.11 = (s32[]{:T(128)}, bf16[4,4,256,128]{3,2,1,0:T(8,128)(2,1)S(1)}, bf16[4,4,256,128]{2,3,1,0:T(8,128)(2,1)S(1)}, bf16[4,1280,128]{2,1,0:T(8,128)(2,1)S(1...) while((s32[]{:T(128)}, ...), condition=%wide.region_8.9_spmd.clone, body=%wide.region_5.8_spmd.clone.sunk | while | flops 681506816 | bytes 17593436 | solution.py:84
  173.9 2.0 %fusion.48 = bf16[4,4,256,128]{3,2,1,0:T(8,128)(2,1)S(1)} fusion(bf16[4,4,256,128]{3,2,1,0:T(8,128)(2,1)S(1)} %get-tuple-element.166, s32[]{:T(128)} %get-tuple-element.165, f32[4,256,1280]{2,1,0:T(8,128)S(1)} %get-tuple-element.154, f32[4,256]{1,0:T(4,128)S(1)} %get-tuple-element.155, bf16[4,1280,128]{2,1,0:T(8,128)(2,1)} %get-tuple-element.178, ...), kind=kOutput, calls=%fused_computation.11.clone.1 | convolution fusion | flops 338427904 | bytes 5841920 | tf_op jit(solution)/shard_map/while/body/eval_jaxpr/dot_general | solution.py:80
  176.2 1.3 fusion.46
  178.5 2.0 %fusion.48 = bf16[4,4,256,128]{3,2,1,0:T(8,128)(2,1)S(1)} fusion(bf16[4,4,256,128]{3,2,1,0:T(8,128)(2,1)S(1)} %get-tuple-element.166, s32[]{:T(128)} %get-tuple-element.165, f32[4,256,1280]{2,1,0:T(8,128)S(1)} %get-tuple-element.154, f32[4,256]{1,0:T(4,128)S(1)} %get-tuple-element.155, bf16[4,1280,128]{2,1,0:T(8,128)(2,1)} %get-tuple-element.178, ...), kind=kOutput, calls=%fused_computation.11.clone.1 | convolution fusion | flops 338427904 | bytes 5841920 | tf_op jit(solution)/shard_map/while/body/eval_jaxpr/dot_general | solution.py:80
  180.8 1.3 fusion.46
  183.1 2.0 %fusion.48 = bf16[4,4,256,128]{3,2,1,0:T(8,128)(2,1)S(1)} fusion(bf16[4,4,256,128]{3,2,1,0:T(8,128)(2,1)S(1)} %get-tuple-element.166, s32[]{:T(128)} %get-tuple-element.165, f32[4,256,1280]{2,1,0:T(8,128)S(1)} %get-tuple-element.154, f32[4,256]{1,0:T(4,128)S(1)} %get-tuple-element.155, bf16[4,1280,128]{2,1,0:T(8,128)(2,1)} %get-tuple-element.178, ...), kind=kOutput, calls=%fused_computation.11.clone.1 | convolution fusion | flops 338427904 | bytes 5841920 | tf_op jit(solution)/shard_map/while/body/eval_jaxpr/dot_general | solution.py:80
  185.5 1.3 fusion.46
  187.7 2.0 %fusion.48 = bf16[4,4,256,128]{3,2,1,0:T(8,128)(2,1)S(1)} fusion(bf16[4,4,256,128]{3,2,1,0:T(8,128)(2,1)S(1)} %get-tuple-element.166, s32[]{:T(128)} %get-tuple-element.165, f32[4,256,1280]{2,1,0:T(8,128)S(1)} %get-tuple-element.154, f32[4,256]{1,0:T(4,128)S(1)} %get-tuple-element.155, bf16[4,1280,128]{2,1,0:T(8,128)(2,1)} %get-tuple-element.178, ...), kind=kOutput, calls=%fused_computation.11.clone.1 | convolution fusion | flops 338427904 | bytes 5841920 | tf_op jit(solution)/shard_map/while/body/eval_jaxpr/dot_general | solution.py:80
  190.6 1.6 reshape.47
  (46 shorter events, 18.9 us)
Async XLA Ops:
  6.5 46.5 %copy-start = (bf16[1,256,2048]{2,1,0:T(8,128)(2,1)S(1)}, bf16[1,256,2048]{2,1,0:T(8,128)(2,1)}, u32[]{:S(2)}) copy-start(bf16[1,256,2048]{2,1,0:T(8,128)(2,1)} %param.8) | copy-start | bytes 3145732
  6.5 44.3 %all-reduce.3.cloned.1.call-start = ((), (), s32[]{:S(2)}) async-start(), calls=%async_computation.2 | async-start | bytes 1048576 | tf_op jit(solution)/shard_map/psum | solution.py:12
  11.1 70.9 %all-gather.3.cloned.1.call-start = ((), (), s32[]{:S(2)}) async-start(), calls=%async_computation | async-start | bytes 2359296 | tf_op jit(solution)/shard_map/all_gather | solution.py:50
  50.8 61.0 %all-gather.5.cloned.1.call-start = ((), (), s32[]{:S(2)}) async-start(), calls=%async_computation.1 | async-start | bytes 2359296 | tf_op jit(solution)/shard_map/all_gather | solution.py:55
  84.3 37.3 %copy-start.4 = (s32[1,4]{1,0:T(1,128)S(1)}, s32[1,4]{1,0:T(1,128)}, u32[]{:S(2)}) copy-start(s32[1,4]{1,0:T(1,128)} %param.13) | copy-start | bytes 52
  84.3 42.1 %copy-start.1 = (bf16[1,256,2048]{2,1,0:T(8,128)(2,1)S(1)}, bf16[1,256,2048]{2,1,0:T(8,128)(2,1)}, u32[]{:S(2)}) copy-start(bf16[1,256,2048]{2,1,0:T(8,128)(2,1)} %param.9) | copy-start | bytes 3145732
  114.2 0.7 copy-start.2
  115.7 36.8 %collective-permute-start = (bf16[2,256,512]{2,1,0:T(8,128)(2,1)}, bf16[2,256,512]{2,1,0:T(8,128)(2,1)}, u32[]{:S(2)}, u32[]{:S(2)}) collective-permute-start(bf16[2,256,512]{2,1,0:T(8,128)(2,1)} %pad_maximum_fusion), channel_id=1, source_target_pairs={{0,16},{4,20},{8,24},{12,28},{1,17},{5,21},{9,25},{13,29},{2,18},{... | collective-permute-start | bytes 1572872 | tf_op jit(solution)/shard_map/ppermute | solution.py:18
  119.5 39.3 %collective-permute-start.1 = (bf16[2,256,512]{2,1,0:T(8,128)(2,1)}, bf16[2,256,512]{2,1,0:T(8,128)(2,1)}, u32[]{:S(2)}, u32[]{:S(2)}) collective-permute-start(bf16[2,256,512]{2,1,0:T(8,128)(2,1)} %pad_maximum_fusion), channel_id=1, source_target_pairs={{0,12},{4,16},{8,20},{12,24},{16,28},{1,13},{5,17},{9,21},{13,25},... | collective-permute-start | bytes 1572872 | tf_op jit(solution)/shard_map/ppermute | solution.py:18
  121.6 38.3 %collective-permute-start.2 = (bf16[2,256,512]{2,1,0:T(8,128)(2,1)}, bf16[2,256,512]{2,1,0:T(8,128)(2,1)}, u32[]{:S(2)}, u32[]{:S(2)}) collective-permute-start(bf16[2,256,512]{2,1,0:T(8,128)(2,1)} %pad_maximum_fusion), channel_id=1, source_target_pairs={{0,8},{4,12},{8,16},{12,20},{16,24},{20,28},{1,9},{5,13},{9,17},{1... | collective-permute-start | bytes 1572872 | tf_op jit(solution)/shard_map/ppermute | solution.py:18
  124.5 36.5 %collective-permute-start.3 = (bf16[2,256,512]{2,1,0:T(8,128)(2,1)}, bf16[2,256,512]{2,1,0:T(8,128)(2,1)}, u32[]{:S(2)}, u32[]{:S(2)}) collective-permute-start(bf16[2,256,512]{2,1,0:T(8,128)(2,1)} %pad_maximum_fusion), channel_id=1, source_target_pairs={{0,4},{4,8},{8,12},{12,16},{16,20},{20,24},{24,28},{1,5},{5,9},{9,... | collective-permute-start | bytes 1572872 | tf_op jit(solution)/shard_map/ppermute | solution.py:18
  127.1 35.0 %copy-start.3 = (bf16[1,256,512]{2,1,0:T(8,128)(2,1)S(1)}, bf16[1,256,512]{2,1,0:T(8,128)(2,1)}, u32[]{:S(2)}) copy-start(bf16[1,256,512]{2,1,0:T(8,128)(2,1)} %copy-done.2) | copy-start | bytes 786436
Sparse Core Ops, SparseCore 0:
  11.2 39.5 all-reduce.2
  52.7 29.2 all-gather.2
  83.9 27.8 all-gather.4
where the time goes:
time: 199 us
  waiting for transfers between devices  127 us (64%)
  local copies, waits for them, and re-layouts  18.5 us (9%)
  matrix products  17.9 us (9%)
  between operations  14.6 us (7%)
  starting transfers between devices  10.8 us (5%)
  other arithmetic  9.72 us (5%)
    psum x1, waiting for transfers between devices, from_root(): return lax.psum(block, axis)  39.7 us
    ppermute x4, waiting for transfers between devices, from_behind(): return lax.ppermute(x, axis, pairs)  30.6 us
    all_gather x1, waiting for transfers between devices, local(): lax.all_gather(key_part, 'ctx', axis=0, tiled=True)  28.6 us
    all_gather x1, waiting for transfers between devices, local(): lax.all_gather(value_part, 'ctx', axis=0, tiled=True)  27.5 us
    ppermute x4, starting transfers between devices, from_behind(): return lax.ppermute(x, axis, pairs)  10.7 us
    dot_general x4, matrix products, one_head(): summed = jnp.dot(weight_b, v_one, preferred_element_type=jnp.float32)  8.07 us
    unnamed x15, local copies, waits for them, and re-layouts  5.55 us
    dot_general x4, matrix products, one_head(): score = jnp.dot(rows, k_one.T, preferred_element_type=jnp.float32)  5.14 us
  transfers between devices with their start and end apart: 7, of which 5 were waited for; matrix products, arithmetic and copies ran while one was open for 4% of the time, Pallas kernels for 0%

commit v1 on v0

--- a/solution.py
+++ b/solution.py
@@ -5,6 +5,18 @@
 
 HS = 128
 REACH = 4
+
+
+def gather_by_bits(array, axis, dim):
+    ways, here = (lax.axis_size(axis), lax.axis_index(axis))
+    grown, reach = (array, 1)
+    while reach < ways:
+        theirs = lax.ppermute(grown, axis, [(d, d ^ reach) for d in range(ways)])
+        mine_first = jnp.concatenate([grown, theirs], axis=dim)
+        theirs_first = jnp.concatenate([theirs, grown], axis=dim)
+        grown = jnp.where(here & reach == 0, mine_first, theirs_first)
+        reach = 2 * reach
+    return grown
 
 
 def from_root(block, axis, owner):
@@ -46,9 +58,7 @@
     key_part = copy_owner(own_slot, owners[0])
     value_part = copy_owner(own_slot, owners[1])
     key_sum = jnp.dot(
-        scaled,
-        lax.all_gather(key_part, "ctx", axis=0, tiled=True),
-        preferred_element_type=jnp.float32,
+        scaled, gather_by_bits(key_part, "ctx", 0), preferred_element_type=jnp.float32
     )
     value_sum = jnp.dot(
         scaled,

time: 199 us -> 190 us (0.955)
  waiting for transfers between devices: 127 us -> 110 us
  starting transfers between devices: 10.8 us -> 17.7 us
    ppermute x0 -> x3, waiting for transfers between devices: none -> 43.6 us  [gather_by_bits(): theirs = lax.ppermute(grown, axis, [(d, d ^ reach) for d in range(ways)])]
    all_gather x1 -> x0, waiting for transfers between devices: 28.6 us -> none  [local(): lax.all_gather(key_part, 'ctx', axis=0, tiled=True)]
    all_gather x1, waiting for transfers between devices: 27.5 us -> 0.02 us  [local(): lax.all_gather(value_part, 'ctx', axis=0, tiled=True)]
    ppermute x0 -> x3, starting transfers between devices: none -> 4.3 us  [gather_by_bits(): theirs = lax.ppermute(grown, axis, [(d, d ^ reach) for d in range(ways)])]
    ppermute x4, waiting for transfers between devices: 30.6 us -> 26.9 us  [from_behind(): return lax.ppermute(x, axis, pairs)]
    ppermute x4, starting transfers between devices: 10.7 us -> 13.3 us  [from_behind(): return lax.ppermute(x, axis, pairs)]
  transfers between devices with their start and end apart: 7 -> 9, of which waited for: 5 -> 6; matrix products, arithmetic and copies ran while one was open for 4% -> 5% of each run, Pallas kernels for 0% -> 0%
where the time goes in v1:
time: 190 us; the launch traced here: 189 us
  waiting for transfers between devices  110 us (58%)
  local copies, waits for them, and re-layouts  18.7 us (10%)
  matrix products  18.1 us (10%)
  starting transfers between devices  17.7 us (9%)
  between operations  14.9 us (8%)
  other arithmetic  9.22 us (5%)
    ppermute x3, waiting for transfers between devices, gather_by_bits(): theirs = lax.ppermute(grown, axis, [(d, d ^ reach) for d in range(ways)])  43.6 us
    psum x1, waiting for transfers between devices, from_root(): return lax.psum(block, axis)  39.7 us
    ppermute x4, waiting for transfers between devices, from_behind(): return lax.ppermute(x, axis, pairs)  26.9 us
    ppermute x4, starting transfers between devices, from_behind(): return lax.ppermute(x, axis, pairs)  13.3 us
    dot_general x4, matrix products, one_head(): summed = jnp.dot(weight_b, v_one, preferred_element_type=jnp.float32)  8.07 us
    unnamed x15, local copies, waits for them, and re-layouts  5.81 us
    dot_general x4, matrix products, one_head(): score = jnp.dot(rows, k_one.T, preferred_element_type=jnp.float32)  5.14 us
    ppermute x3, starting transfers between devices, gather_by_bits(): theirs = lax.ppermute(grown, axis, [(d, d ^ reach) for d in range(ways)])  4.3 us
  transfers between devices with their start and end apart: 9, of which 6 were waited for; matrix products, arithmetic and copies ran while one was open for 5% of the time, Pallas kernels for 0%

profile of v1, /device:TPU:1, one launch (start us, length us, event | category | flops | bytes accessed | tf_op | source)
XLA Modules:
  0.0 188.9 jit_solution(4720363850718230239)
XLA Ops:
  6.5 1.4 fusion.45
  9.3 1.8 select_bitcast_fusion.1
  11.1 39.7 %all-reduce.3.cloned.1.call-done = (bf16[256,512]{1,0:T(8,128)(2,1)}, bf16[256,512]{1,0:T(8,128)(2,1)}) async-done(((bf16[256,512]{1,0:T(8,128)(2,1)}, bf16[256,512]{1,0:T(8,128)(2,1)}), (bf16[256,512]{1,0:T(8,128)(2,1)}, bf16[256,512]{1,0:T(8,128)(2,1)})) %all-reduce.3.cloned.1.call-update) | async-done | bytes 524304 | tf_op jit(solution)/shard_map/psum | solution.py:24
  50.8 1.7 collective-permute-start
  52.6 1.4 collective-permute-done
  56.4 14.7 %collective-permute-done.1 = bf16[512,512]{1,0:T(8,128)(2,1)S(1)} collective-permute-done((bf16[512,512]{1,0:T(8,128)(2,1)S(1)}, bf16[512,512]{1,0:T(8,128)(2,1)S(1)}, u32[]{:S(2)}, u32[]{:S(2)}) %collective-permute-start.1) | collective-permute-done | bytes 524320 | tf_op jit(solution)/shard_map/ppermute | solution.py:14
  73.3 27.5 %collective-permute-done.2 = bf16[1024,512]{1,0:T(8,128)(2,1)} collective-permute-done((bf16[1024,512]{1,0:T(8,128)(2,1)S(1)}, bf16[1024,512]{1,0:T(8,128)(2,1)}, u32[]{:S(2)}, u32[]{:S(2)}) %collective-permute-start.2) | collective-permute-done | bytes 1048608 | tf_op jit(solution)/shard_map/ppermute | solution.py:14
  100.8 2.4 %fusion.38 = bf16[1,256,512]{2,1,0:T(8,128)(2,1)S(1)} fusion(bf16[1024,512]{1,0:T(8,128)(2,1)} %collective-permute-done.2, bf16[1024,512]{1,0:T(8,128)(2,1)S(1)} %maximum_select_fusion.6, pred[]{:T(512)S(6)} %eq.15, bf16[1,256,2048]{2,1,0:T(8,128)(2,1)S(1)} %copy-done, f32[2048]{0:T(1024)S(1)} %convert_element_type.26, f32[256]{0:T(256)S(1)} %add_rsqrt_fusion), kind=kOutput, calls=%fused_computation.37 | convolution fusion | flops 548536320 | bytes 3417089 | tf_op jit(solution)/shard_map/dot_general | solution.py:60
  103.3 2.4 %fusion.39 = bf16[1,256,512]{2,1,0:T(8,128)(2,1)S(1)} fusion(bf16[2048,512]{1,0:T(8,128)(2,1)} %all-gather.2.cloned.1.call-done, bf16[1,256,2048]{2,1,0:T(8,128)(2,1)S(1)} %copy-done, f32[2048]{0:T(1024)S(1)} %convert_element_type.26, f32[256]{0:T(256)S(1)} %add_rsqrt_fusion), kind=kOutput, calls=%fused_computation.38 | convolution fusion | flops 539099136 | bytes 3417088 | tf_op jit(solution)/shard_map/dot_general | solution.py:63
  105.8 3.9 %collective-permute-start.3 = (bf16[2,256,512]{2,1,0:T(8,128)(2,1)S(1)}, bf16[2,256,512]{2,1,0:T(8,128)(2,1)}, u32[]{:S(2)}, u32[]{:S(2)}) collective-permute-start(bf16[2,256,512]{2,1,0:T(8,128)(2,1)S(1)} %pad_maximum_fusion), channel_id=1, source_target_pairs={{0,16},{4,20},{8,24},{12,28},{1,17},{5,21},{9,25},{13,29},{2,18},{... | collective-permute-start | bytes 1572872 | tf_op jit(solution)/shard_map/ppermute | solution.py:30
  109.7 3.3 %collective-permute-start.4 = (bf16[2,256,512]{2,1,0:T(8,128)(2,1)S(1)}, bf16[2,256,512]{2,1,0:T(8,128)(2,1)}, u32[]{:S(2)}, u32[]{:S(2)}) collective-permute-start(bf16[2,256,512]{2,1,0:T(8,128)(2,1)S(1)} %pad_maximum_fusion), channel_id=1, source_target_pairs={{0,12},{4,16},{8,20},{12,24},{16,28},{1,13},{5,17},{9,21},{13,25},... | collective-permute-start | bytes 1572872 | tf_op jit(solution)/shard_map/ppermute | solution.py:30
  113.0 3.1 %collective-permute-start.5 = (bf16[2,256,512]{2,1,0:T(8,128)(2,1)S(1)}, bf16[2,256,512]{2,1,0:T(8,128)(2,1)}, u32[]{:S(2)}, u32[]{:S(2)}) collective-permute-start(bf16[2,256,512]{2,1,0:T(8,128)(2,1)S(1)} %pad_maximum_fusion), channel_id=1, source_target_pairs={{0,8},{4,12},{8,16},{12,20},{16,24},{20,28},{1,9},{5,13},{9,17},{1... | collective-permute-start | bytes 1572872 | tf_op jit(solution)/shard_map/ppermute | solution.py:30
  116.1 3.0 %collective-permute-start.6 = (bf16[2,256,512]{2,1,0:T(8,128)(2,1)S(1)}, bf16[2,256,512]{2,1,0:T(8,128)(2,1)}, u32[]{:S(2)}, u32[]{:S(2)}) collective-permute-start(bf16[2,256,512]{2,1,0:T(8,128)(2,1)S(1)} %pad_maximum_fusion), channel_id=1, source_target_pairs={{0,4},{4,8},{8,12},{12,16},{16,20},{20,24},{24,28},{1,5},{5,9},{9,... | collective-permute-start | bytes 1572872 | tf_op jit(solution)/shard_map/ppermute | solution.py:30
  119.1 1.5 copy.15
  120.7 19.7 %collective-permute-done.3 = bf16[2,256,512]{2,1,0:T(8,128)(2,1)} collective-permute-done((bf16[2,256,512]{2,1,0:T(8,128)(2,1)S(1)}, bf16[2,256,512]{2,1,0:T(8,128)(2,1)}, u32[]{:S(2)}, u32[]{:S(2)}) %collective-permute-start.3) | collective-permute-done | bytes 524320 | tf_op jit(solution)/shard_map/ppermute | solution.py:30
  141.5 7.2 %collective-permute-done.4 = bf16[2,256,512]{2,1,0:T(8,128)(2,1)} collective-permute-done((bf16[2,256,512]{2,1,0:T(8,128)(2,1)S(1)}, bf16[2,256,512]{2,1,0:T(8,128)(2,1)}, u32[]{:S(2)}, u32[]{:S(2)}) %collective-permute-start.4) | collective-permute-done | bytes 524320 | tf_op jit(solution)/shard_map/ppermute | solution.py:30
  153.3 3.6 %reshape_squeeze.10 = bf16[1280,4,128]{2,1,0:T(4,128)(2,1)} reshape(bf16[1,1280,512]{2,1,0:T(8,128)(2,1)} %get-tuple-element.96) | data formatting | bytes 2621440 | tf_op jit(solution)/shard_map/reshape;squeeze | solution.py:76
  158.1 3.1 %copy_bitcast_fusion = (bf16[4,1280,128]{2,1,0:T(8,128)(2,1)}, bf16[4,1280,128]{2,1,0:T(8,128)(2,1)S(1)}) fusion(bf16[1280,4,128]{2,1,0:T(4,128)(2,1)} %reshape_squeeze.11, bf16[1280,4,128]{2,1,0:T(4,128)(2,1)} %reshape_squeeze.10), kind=kLoop, calls=%fused_computation.33 | loop fusion | bytes 5242880 | tf_op jit(solution)/shard_map/transpose | solution.py:77
  161.2 18.5 %while.11 = (s32[]{:T(128)}, bf16[4,4,256,128]{3,2,1,0:T(8,128)(2,1)S(1)}, bf16[4,4,256,128]{2,3,1,0:T(8,128)(2,1)S(1)}, bf16[4,1280,128]{2,1,0:T(8,128)(2,1)S(1...) while((s32[]{:T(128)}, ...), condition=%wide.region_8.9_spmd.clone, body=%wide.region_5.8_spmd.clone.sunk | while | flops 681506816 | bytes 17593436 | solution.py:94
  163.8 2.0 %fusion.56 = bf16[4,4,256,128]{3,2,1,0:T(8,128)(2,1)S(1)} fusion(bf16[4,4,256,128]{3,2,1,0:T(8,128)(2,1)S(1)} %get-tuple-element.166, s32[]{:T(128)} %get-tuple-element.165, f32[4,256,1280]{2,1,0:T(8,128)S(1)} %get-tuple-element.154, f32[4,256]{1,0:T(4,128)S(1)} %get-tuple-element.155, bf16[4,1280,128]{2,1,0:T(8,128)(2,1)} %get-tuple-element.178, ...), kind=kOutput, calls=%fused_computation.11.clone.1 | convolution fusion | flops 338427904 | bytes 5841920 | tf_op jit(solution)/shard_map/while/body/eval_jaxpr/dot_general | solution.py:90
  168.4 2.0 %fusion.56 = bf16[4,4,256,128]{3,2,1,0:T(8,128)(2,1)S(1)} fusion(bf16[4,4,256,128]{3,2,1,0:T(8,128)(2,1)S(1)} %get-tuple-element.166, s32[]{:T(128)} %get-tuple-element.165, f32[4,256,1280]{2,1,0:T(8,128)S(1)} %get-tuple-element.154, f32[4,256]{1,0:T(4,128)S(1)} %get-tuple-element.155, bf16[4,1280,128]{2,1,0:T(8,128)(2,1)} %get-tuple-element.178, ...), kind=kOutput, calls=%fused_computation.11.clone.1 | convolution fusion | flops 338427904 | bytes 5841920 | tf_op jit(solution)/shard_map/while/body/eval_jaxpr/dot_general | solution.py:90
  173.0 2.0 %fusion.56 = bf16[4,4,256,128]{3,2,1,0:T(8,128)(2,1)S(1)} fusion(bf16[4,4,256,128]{3,2,1,0:T(8,128)(2,1)S(1)} %get-tuple-element.166, s32[]{:T(128)} %get-tuple-element.165, f32[4,256,1280]{2,1,0:T(8,128)S(1)} %get-tuple-element.154, f32[4,256]{1,0:T(4,128)S(1)} %get-tuple-element.155, bf16[4,1280,128]{2,1,0:T(8,128)(2,1)} %get-tuple-element.178, ...), kind=kOutput, calls=%fused_computation.11.clone.1 | convolution fusion | flops 338427904 | bytes 5841920 | tf_op jit(solution)/shard_map/while/body/eval_jaxpr/dot_general | solution.py:90
  177.6 2.0 %fusion.56 = bf16[4,4,256,128]{3,2,1,0:T(8,128)(2,1)S(1)} fusion(bf16[4,4,256,128]{3,2,1,0:T(8,128)(2,1)S(1)} %get-tuple-element.166, s32[]{:T(128)} %get-tuple-element.165, f32[4,256,1280]{2,1,0:T(8,128)S(1)} %get-tuple-element.154, f32[4,256]{1,0:T(4,128)S(1)} %get-tuple-element.155, bf16[4,1280,128]{2,1,0:T(8,128)(2,1)} %get-tuple-element.178, ...), kind=kOutput, calls=%fused_computation.11.clone.1 | convolution fusion | flops 338427904 | bytes 5841920 | tf_op jit(solution)/shard_map/while/body/eval_jaxpr/dot_general | solution.py:90
  180.5 1.6 reshape.47
  (51 shorter events, 22.8 us)
Async XLA Ops:
  6.5 44.2 %all-reduce.3.cloned.1.call-start = ((), (), s32[]{:S(2)}) async-start(), calls=%async_computation.1 | async-start | bytes 1048576 | tf_op jit(solution)/shard_map/psum | solution.py:24
  11.0 61.8 %copy-start.3 = (bf16[2048]{0:T(1024)(128)(2,1)S(1)}, bf16[2048]{0:T(1024)(128)(2,1)}, u32[]{:S(2)}) copy-start(bf16[2048]{0:T(1024)(128)(2,1)} %param.10) | copy-start | bytes 12292
  11.0 61.8 %copy-start.4 = (s32[1,4]{1,0:T(1,128)S(1)}, s32[1,4]{1,0:T(1,128)}, u32[]{:S(2)}) copy-start(s32[1,4]{1,0:T(1,128)} %param.13) | copy-start | bytes 52
  11.0 62.0 %copy-start = (bf16[1,256,2048]{2,1,0:T(8,128)(2,1)S(1)}, bf16[1,256,2048]{2,1,0:T(8,128)(2,1)}, u32[]{:S(2)}) copy-start(bf16[1,256,2048]{2,1,0:T(8,128)(2,1)} %param.8) | copy-start | bytes 3145732
  11.1 92.2 %all-gather.2.cloned.1.call-start = ((), (), s32[]{:S(2)}) async-start(), calls=%async_computation | async-start | bytes 2359296 | tf_op jit(solution)/shard_map/all_gather | solution.py:65
  50.8 3.1 %collective-permute-start = (bf16[256,512]{1,0:T(8,128)(2,1)}, bf16[256,512]{1,0:T(8,128)(2,1)S(1)}, u32[]{:S(2)}, u32[]{:S(2)}) collective-permute-start(bf16[256,512]{1,0:T(8,128)(2,1)} %get-tuple-element.92), channel_id=1, source_target_pairs={{0,4},{4,0},{8,12},{12,8},{16,20},{20,16},{24,28},{28,24},{1,5},{5... | collective-permute-start | bytes 786440 | tf_op jit(solution)/shard_map/ppermute | solution.py:14
  55.1 16.0 %collective-permute-start.1 = (bf16[512,512]{1,0:T(8,128)(2,1)S(1)}, bf16[512,512]{1,0:T(8,128)(2,1)S(1)}, u32[]{:S(2)}, u32[]{:S(2)}) collective-permute-start(bf16[512,512]{1,0:T(8,128)(2,1)S(1)} %maximum_select_fusion.7), channel_id=1, source_target_pairs={{0,8},{4,12},{8,0},{12,4},{16,24},{20,28},{24,16},{28,20},{1,9},{5... | collective-permute-start | bytes 1572872 | tf_op jit(solution)/shard_map/ppermute | solution.py:14
  71.6 29.2 %collective-permute-start.2 = (bf16[1024,512]{1,0:T(8,128)(2,1)S(1)}, bf16[1024,512]{1,0:T(8,128)(2,1)}, u32[]{:S(2)}, u32[]{:S(2)}) collective-permute-start(bf16[1024,512]{1,0:T(8,128)(2,1)S(1)} %maximum_select_fusion.6), channel_id=1, source_target_pairs={{0,16},{4,20},{8,24},{12,28},{16,0},{20,4},{24,8},{28,12},{1,17},{... | collective-permute-start | bytes 3145736 | tf_op jit(solution)/shard_map/ppermute | solution.py:14
  103.2 2.5 %copy-start.1 = (bf16[1,256,512]{2,1,0:T(8,128)(2,1)}, bf16[1,256,512]{2,1,0:T(8,128)(2,1)S(1)}, u32[]{:S(2)}) copy-start(bf16[1,256,512]{2,1,0:T(8,128)(2,1)S(1)} %fusion.38) | copy-start | bytes 786436
  105.8 34.7 %collective-permute-start.3 = (bf16[2,256,512]{2,1,0:T(8,128)(2,1)S(1)}, bf16[2,256,512]{2,1,0:T(8,128)(2,1)}, u32[]{:S(2)}, u32[]{:S(2)}) collective-permute-start(bf16[2,256,512]{2,1,0:T(8,128)(2,1)S(1)} %pad_maximum_fusion), channel_id=1, source_target_pairs={{0,16},{4,20},{8,24},{12,28},{1,17},{5,21},{9,25},{13,29},{2,18},{... | collective-permute-start | bytes 1572872 | tf_op jit(solution)/shard_map/ppermute | solution.py:30
  109.7 39.0 %collective-permute-start.4 = (bf16[2,256,512]{2,1,0:T(8,128)(2,1)S(1)}, bf16[2,256,512]{2,1,0:T(8,128)(2,1)}, u32[]{:S(2)}, u32[]{:S(2)}) collective-permute-start(bf16[2,256,512]{2,1,0:T(8,128)(2,1)S(1)} %pad_maximum_fusion), channel_id=1, source_target_pairs={{0,12},{4,16},{8,20},{12,24},{16,28},{1,13},{5,17},{9,21},{13,25},... | collective-permute-start | bytes 1572872 | tf_op jit(solution)/shard_map/ppermute | solution.py:30
  113.0 36.8 %collective-permute-start.5 = (bf16[2,256,512]{2,1,0:T(8,128)(2,1)S(1)}, bf16[2,256,512]{2,1,0:T(8,128)(2,1)}, u32[]{:S(2)}, u32[]{:S(2)}) collective-permute-start(bf16[2,256,512]{2,1,0:T(8,128)(2,1)S(1)} %pad_maximum_fusion), channel_id=1, source_target_pairs={{0,8},{4,12},{8,16},{12,20},{16,24},{20,28},{1,9},{5,13},{9,17},{1... | collective-permute-start | bytes 1572872 | tf_op jit(solution)/shard_map/ppermute | solution.py:30
  116.1 34.7 %collective-permute-start.6 = (bf16[2,256,512]{2,1,0:T(8,128)(2,1)S(1)}, bf16[2,256,512]{2,1,0:T(8,128)(2,1)}, u32[]{:S(2)}, u32[]{:S(2)}) collective-permute-start(bf16[2,256,512]{2,1,0:T(8,128)(2,1)S(1)} %pad_maximum_fusion), channel_id=1, source_target_pairs={{0,4},{4,8},{8,12},{12,16},{16,20},{20,24},{24,28},{1,5},{5,9},{9,... | collective-permute-start | bytes 1572872 | tf_op jit(solution)/shard_map/ppermute | solution.py:30
  120.7 31.3 %copy-start.2 = (bf16[1,256,512]{2,1,0:T(8,128)(2,1)S(1)}, bf16[1,256,512]{2,1,0:T(8,128)(2,1)}, u32[]{:S(2)}) copy-start(bf16[1,256,512]{2,1,0:T(8,128)(2,1)} %copy-done.1) | copy-start | bytes 786436
Sparse Core Ops, SparseCore 0:
  11.2 39.5 all-reduce.2
  52.7 37.7 all-gather.1
